TPU v7x, 256 devices: a whole 4x4x8 slice. The times are simulated.
256 devices in a mesh: feat: 16 (over z, core), dom: 16 (over x, y).
Axes of the slice: x: 4, y: 4, z: 8, core: 2. Of those that a mesh axis runs over, the one named last changes fastest.
Arguments:
- features: bfloat16 [16, 1024, 9216], P('dom', 'feat'), may hold values from -6 to 6
- w1_self: bfloat16 [1024, 256], P('feat'), may hold values from -0.1875 to 0.1875
- w1_neigh: bfloat16 [1024, 256], P('feat'), may hold values from -0.1875 to 0.1875
- w2_self: bfloat16 [256, 256], replicated, may hold values from -0.375 to 0.375
- w2_neigh: bfloat16 [256, 256], replicated, may hold values from -0.375 to 0.375
- neigh_one: int32 [16, 10, 4608], P('dom'), may hold values from 0 to 9215
- send_rows: int32 [16, 16, 16, 128], P('dom', 'feat'), may hold values from 0 to 287
- recv_count: int32 [16, 16, 16], P(None, 'feat', 'dom'), may hold values from 1 to 128, as said below
- neigh_two: int32 [16, 16, 256, 15], P('dom', 'feat'), may hold values from 0 to 2047, as said below
- seed_rows: int32 [16, 16, 256], P('dom', 'feat'), may hold values from 0 to 287, as said below
- d_out: bfloat16 [16, 16, 256, 256], P('dom', 'feat'), may hold values from -0.0625 to 0.0625
Outputs:
- layer_two: bfloat16 [16, 16, 256, 256], P('dom', 'feat')
- grad_w1_self: float32 [1024, 256], P('feat')
- grad_w1_neigh: float32 [1024, 256], P('feat')
- grad_w2_self: float32 [256, 256], replicated
- grad_w2_neigh: float32 [256, 256], replicated
Inputs may be any that keep to these rules, and one draw needn't show every extreme that they name: `neigh_one`: columns of the partition's 9216 input nodes. `send_rows`: rows among the sending device's 288 owned nodes. `recv_count`: the live slots of a buffer are its leading ones; every receiver gets a full buffer of 128 live rows from some source, and some receiver gets full buffers from every source. `neigh_two`: each is below the total of the receiving device's counts; on every device some seed names the last live row. `seed_rows`: distinct within one device.
All inputs are finite; a program needn't handle non-finite values.
Results may differ from a plain program's by a relative error of at most 0.0051.
Values may be sent and summed in bfloat16 or wider, within the bound.
No kernel may reach another device: no remote copies, remote signals or barrier semaphores. Data moves between devices by JAX's collectives and lax.ppermute only.
A program may use at most 64 MiB of HBM per device.

v0:
```python
import jax
import jax.numpy as jnp
from jax import lax
from jax.sharding import PartitionSpec as P


def rows_of(source_table, index_rows):
    return jnp.take(source_table, index_rows, axis=0)


def contract_rows(left_side, right_side):
    return lax.dot_general(
        left_side, right_side, (((0,), (0,)), ((), ())), preferred_element_type=jnp.float32
    )


def contract_cols(left_side, right_side):
    return lax.dot_general(
        left_side, right_side, (((1,), (1,)), ((), ())), preferred_element_type=jnp.float32
    )


def per_device(
    features,
    w1_self,
    w1_neigh,
    w2_self,
    w2_neigh,
    neigh_one,
    send_rows,
    recv_count,
    neigh_two,
    seed_rows,
    d_out,
):
    feature_table = features[0]
    neigh_lists = neigh_one[0]
    target_rows = neigh_lists.shape[1]
    fan_one = neigh_lists.shape[0]
    running = jnp.zeros((feature_table.shape[0], target_rows), jnp.float32)
    for column in range(fan_one):
        running = running + jnp.take(feature_table, neigh_lists[column], axis=1).astype(jnp.float32)
    mean_one = (running / fan_one).astype(jnp.bfloat16)
    own_self = feature_table[:, :target_rows]
    owned_rows = target_rows // lax.axis_size("feat")
    hidden_width = w1_self.shape[1]
    left_self = own_self
    left_mean = mean_one
    pre_one = lax.psum_scatter(
        contract_rows(left_self, w1_self) + contract_rows(left_mean, w1_neigh),
        "feat",
        scatter_dimension=0,
        tiled=True,
    )
    hidden = jax.nn.elu(pre_one).astype(jnp.bfloat16)
    send_index = send_rows[0, 0]
    peer_count = send_index.shape[0]
    slot_count = send_index.shape[1]
    outgoing = rows_of(hidden, send_index.reshape(-1)).reshape(peer_count, slot_count, hidden_width)
    incoming = lax.all_to_all(outgoing, "dom", split_axis=0, concat_axis=0, tiled=True)
    flat_in = incoming.reshape(peer_count * slot_count, hidden_width)
    counts = recv_count[:, 0, 0]
    starts = jnp.cumsum(counts) - counts
    positions = neigh_two[0, 0]
    source = jnp.sum((positions[:, :, None] >= starts[None, None, 1:]).astype(jnp.int32), axis=2)
    picked = (source[:, :, None] == jnp.arange(peer_count, dtype=jnp.int32)).astype(jnp.int32)
    offset_of = jnp.sum(picked * starts[None, None, :], axis=2)
    where_in = source * slot_count + positions - offset_of
    fan_two = positions.shape[1]
    seed_count = positions.shape[0]
    running_two = jnp.zeros((seed_count, hidden_width), jnp.float32)
    for column in range(fan_two):
        running_two = running_two + rows_of(flat_in, where_in[:, column]).astype(jnp.float32)
    mean_two = (running_two / fan_two).astype(jnp.bfloat16)
    seeds = seed_rows[0, 0]
    self_two = rows_of(hidden, seeds)
    grad_out = d_out[0, 0]
    layer_out = (
        jnp.dot(self_two, w2_self, preferred_element_type=jnp.float32)
        + jnp.dot(mean_two, w2_neigh, preferred_element_type=jnp.float32)
    ).astype(jnp.bfloat16)
    local_w2_self = contract_rows(self_two, grad_out)
    local_w2_neigh = contract_rows(mean_two, grad_out)
    d_self = contract_cols(grad_out, w2_self)
    d_mean = contract_cols(grad_out, w2_neigh) / fan_two
    slot_sum = jnp.zeros((peer_count * slot_count, hidden_width), jnp.float32)
    for column in range(fan_two):
        slot_sum = slot_sum.at[where_in[:, column]].add(d_mean)
    slot_grad = slot_sum.astype(jnp.bfloat16).reshape(peer_count, slot_count, hidden_width)
    returned = lax.all_to_all(slot_grad, "dom", split_axis=0, concat_axis=0, tiled=True)
    d_hidden = jnp.zeros((owned_rows, hidden_width), jnp.float32)
    d_hidden = d_hidden.at[send_index.reshape(-1)].add(
        returned.reshape(-1, hidden_width).astype(jnp.float32)
    )
    d_hidden = d_hidden.at[seeds].add(d_self)
    elu_slope = jnp.where(pre_one > 0, 1.0, jnp.exp(jnp.minimum(pre_one, 0.0)))
    d_pre = (d_hidden * elu_slope).astype(jnp.bfloat16)
    piece = lax.all_gather(d_pre, "feat", axis=0, tiled=True)
    left_self = own_self
    left_mean = mean_one
    first_self = jnp.dot(left_self, piece, preferred_element_type=jnp.float32)
    first_mean = jnp.dot(left_mean, piece, preferred_element_type=jnp.float32)
    first_self, first_mean = lax.psum((first_self, first_mean), "dom")
    second_self, second_mean = lax.psum((local_w2_self, local_w2_neigh), ("feat", "dom"))
    return (layer_out[None, None], first_self, first_mean, second_self, second_mean)


def solution(mesh):
    return jax.shard_map(
        per_device,
        mesh=mesh,
        in_specs=(
            P("dom", "feat", None),
            P("feat", None),
            P("feat", None),
            P(),
            P(),
            P("dom", None, None),
            P("dom", "feat", None, None),
            P(None, "feat", "dom"),
            P("dom", "feat", None, None),
            P("dom", "feat", None),
            P("dom", "feat", None, None),
        ),
        out_specs=(P("dom", "feat", None, None), P("feat", None), P("feat", None), P(), P()),
        check_vma=False,
    )
```

profile of v0, /device:TPU:2, one launch (start us, length us, event | category | flops | bytes accessed | tf_op | source)
XLA Modules:
  0.0 690.3 jit_solution(7600817708877585368)
XLA Ops:
  7.2 1.2 slice_reduce_fusion.9
  8.7 2.8 copy.24
  11.5 10.1 %gather_fusion.2 = bf16[4608,64]{1,0:T(8,128)(2,1)} fusion(bf16[64,9216]{0,1:T(8,128)(2,1)S(1)} %bitcast.99, s32[5120]{0:T(1024)S(1)} %pad_clamp_fusion.9), kind=kCustom, calls=%fused_computation.clone | custom fusion | bytes 1198080 | tf_op jit(solution)/shard_map/jit(_take)/gather | solution.py:42
  21.6 10.1 %gather_fusion.3 = bf16[4608,64]{1,0:T(8,128)(2,1)} fusion(bf16[64,9216]{0,1:T(8,128)(2,1)S(1)} %bitcast.100, s32[5120]{0:T(1024)S(1)} %pad_clamp_fusion.8), kind=kCustom, calls=%fused_computation.2.clone | custom fusion | bytes 1198080 | tf_op jit(solution)/shard_map/jit(_take)/gather | solution.py:42
  31.7 10.1 %gather_fusion.4 = bf16[4608,64]{1,0:T(8,128)(2,1)} fusion(bf16[64,9216]{0,1:T(8,128)(2,1)S(1)} %bitcast.101, s32[5120]{0:T(1024)S(1)} %pad_clamp_fusion.7), kind=kCustom, calls=%fused_computation.3.clone | custom fusion | bytes 1198080 | tf_op jit(solution)/shard_map/jit(_take)/gather | solution.py:42
  41.8 10.1 %gather_fusion.5 = bf16[4608,64]{1,0:T(8,128)(2,1)} fusion(bf16[64,9216]{0,1:T(8,128)(2,1)S(1)} %bitcast.102, s32[5120]{0:T(1024)S(1)} %pad_clamp_fusion.6), kind=kCustom, calls=%fused_computation.4.clone | custom fusion | bytes 1198080 | tf_op jit(solution)/shard_map/jit(_take)/gather | solution.py:42
  51.9 10.1 %gather_fusion.6 = bf16[4608,64]{1,0:T(8,128)(2,1)} fusion(bf16[64,9216]{0,1:T(8,128)(2,1)S(1)} %bitcast.103, s32[5120]{0:T(1024)S(1)} %pad_clamp_fusion.5), kind=kCustom, calls=%fused_computation.5.clone | custom fusion | bytes 1198080 | tf_op jit(solution)/shard_map/jit(_take)/gather | solution.py:42
  62.1 10.1 %gather_fusion.7 = bf16[4608,64]{1,0:T(8,128)(2,1)} fusion(bf16[64,9216]{0,1:T(8,128)(2,1)S(1)} %bitcast.104, s32[5120]{0:T(1024)S(1)} %pad_clamp_fusion.4), kind=kCustom, calls=%fused_computation.6.clone | custom fusion | bytes 1198080 | tf_op jit(solution)/shard_map/jit(_take)/gather | solution.py:42
  72.2 10.1 %gather_fusion.8 = bf16[4608,64]{1,0:T(8,128)(2,1)} fusion(bf16[64,9216]{0,1:T(8,128)(2,1)S(1)} %bitcast.105, s32[5120]{0:T(1024)S(1)} %pad_clamp_fusion.3), kind=kCustom, calls=%fused_computation.7.clone | custom fusion | bytes 1198080 | tf_op jit(solution)/shard_map/jit(_take)/gather | solution.py:42
  82.3 10.1 %gather_fusion.9 = bf16[4608,64]{1,0:T(8,128)(2,1)} fusion(bf16[64,9216]{0,1:T(8,128)(2,1)S(1)} %bitcast.106, s32[5120]{0:T(1024)S(1)} %pad_clamp_fusion.2), kind=kCustom, calls=%fused_computation.8.clone | custom fusion | bytes 1198080 | tf_op jit(solution)/shard_map/jit(_take)/gather | solution.py:42
  92.4 10.1 %gather_fusion.10 = bf16[4608,64]{1,0:T(8,128)(2,1)} fusion(bf16[64,9216]{0,1:T(8,128)(2,1)S(1)} %bitcast.107, s32[5120]{0:T(1024)S(1)} %pad_clamp_fusion.1), kind=kCustom, calls=%fused_computation.9.clone | custom fusion | bytes 1198080 | tf_op jit(solution)/shard_map/jit(_take)/gather | solution.py:42
  102.6 10.1 %gather_fusion.11 = bf16[4608,64]{1,0:T(8,128)(2,1)} fusion(bf16[64,9216]{0,1:T(8,128)(2,1)S(1)} %bitcast.108, s32[5120]{0:T(1024)S(1)} %pad_clamp_fusion), kind=kCustom, calls=%fused_computation.10.clone | custom fusion | bytes 1198080 | tf_op jit(solution)/shard_map/jit(_take)/gather | solution.py:42
  116.8 10.3 %multiply_convert_fusion = bf16[64,4608]{0,1:T(8,128)(2,1)S(1)} fusion(bf16[4608,64]{1,0:T(8,128)(2,1)} %gather_fusion.11, bf16[4608,64]{1,0:T(8,128)(2,1)S(1)} %copy-done.11, bf16[4608,64]{1,0:T(8,128)(2,1)S(1)} %copy-done.10, bf16[4608,64]{1,0:T(8,128)(2,1)S(1)} %copy-done.9, bf16[4608,64]{1,0:T(8,128)(2,1)S(1)} %copy-done.8, ...), kind=kLoop, calls=%fused_computation.45 | loop fusion | flops 9142272 | bytes 6534144 | tf_op jit(solution)/shard_map/convert_element_type | solution.py:43
  128.1 2.9 convolution_add_fusion
  133.0 3.4 scatter_custom_fusion
  136.4 4.7 scatter_fusion
  141.2 5.2 scatter_fusion.1
  146.3 4.7 scatter_fusion.2
  151.1 4.8 scatter_fusion.3
  155.8 4.7 scatter_fusion.4
  160.6 4.7 scatter_fusion.5
  165.3 4.8 scatter_fusion.6
  170.1 4.8 scatter_fusion.7
  174.8 4.7 scatter_fusion.8
  179.5 4.8 scatter_fusion.9
  184.3 4.8 scatter_fusion.10
  189.1 4.9 scatter_fusion.11
  194.0 4.7 scatter_fusion.12
  198.7 4.7 scatter_fusion.13
  203.4 2.8 convert_element_type.133
  206.2 7.5 %all-to-all-start.1 = ((bf16[16,128,256]{2,1,0:T(8,128)(2,1)}), bf16[16,128,256]{2,1,0:T(8,128)(2,1)S(1)}, u32[]{:S(2)}, u32[]{:S(2)}) async-start(bf16[16,128,256]{2,1,0:T(8,128)(2,1)} %bitcast.53), calls=%async_computation.2 | async-start | bytes 2097152 | tf_op jit(solution)/shard_map/all_to_all | solution.py:90
  225.6 1.8 fusion.18
  229.7 11.0 %scatter_custom_fusion.15 = f32[288,256]{1,0:T(8,128)S(1)} fusion(s32[2048]{0:T(1024)S(1)} %bitcast.115, bf16[2048,256]{1,0:T(8,128)(2,1)} %bitcast.111, f32[]{:T(128)} %constant.47.clone.1), kind=kCustom, calls=%fused_computation.46 | custom fusion | flops 1048576 | bytes 1343492 | tf_op jit(solution)/shard_map/scatter-add | solution.py:92
  240.9 2.5 scatter_fusion.14
  243.4 1.8 fusion.12
  249.9 9.0 %gather_fusion.1 = bf16[2048,256]{1,0:T(8,128)(2,1)} fusion(bf16[288,256]{1,0:T(8,128)(2,1)S(1)} %get-tuple-element.22, s32[2048]{0:T(1024)S(1)} %broadcast_clamp_fusion), kind=kCustom, calls=%fused_computation.26 | custom fusion | bytes 2105344 | tf_op jit(solution)/shard_map/jit(_take)/gather | solution.py:8
  258.9 2.3 broadcast_select_fusion
  261.2 7.0 %all-to-all-start = ((bf16[16,128,256]{2,1,0:T(8,128)(2,1)}), bf16[16,128,256]{2,1,0:T(8,128)(2,1)}, u32[]{:S(2)}, u32[]{:S(2)}) async-start(bf16[16,128,256]{2,1,0:T(8,128)(2,1)} %broadcast_select_fusion), calls=%async_computation.1 | async-start | bytes 2097152 | tf_op jit(solution)/shard_map/all_to_all | solution.py:60
  270.1 1.1 gather_fusion
  272.5 10.3 %all-to-all-done = bf16[16,128,256]{2,1,0:T(8,128)(2,1)} async-done(((bf16[16,128,256]{2,1,0:T(8,128)(2,1)}), bf16[16,128,256]{2,1,0:T(8,128)(2,1)}, u32[]{:S(2)}, u32[]{:S(2)}) %all-to-all-start) | async-done | bytes 1048608 | tf_op jit(solution)/shard_map/all_to_all | solution.py:60
  282.9 2.5 gather_fusion.23
  285.3 2.5 gather_fusion.24
  287.8 2.5 gather_fusion.25
  290.3 2.5 gather_fusion.26
  292.7 2.5 gather_fusion.12
  295.2 3.1 gather_fusion.13
  298.3 3.1 gather_fusion.14
  301.4 3.1 gather_fusion.15
  304.5 3.1 gather_fusion.16
  307.6 3.1 gather_fusion.17
  310.7 3.1 gather_fusion.18
  313.9 3.1 gather_fusion.19
  317.0 3.1 gather_fusion.20
  320.1 3.1 gather_fusion.21
  323.2 3.1 gather_fusion.22
  326.3 2.1 multiply_convert_fusion.1
  329.4 3.3 fusion.25
  332.7 1.3 convolution_bitcast_fusion
  334.9 247.9 %all-reduce.5.cloned.1.call-done = (f32[256,256]{1,0:T(8,128)}, f32[256,256]{1,0:T(8,128)}) async-done(((f32[256,256]{1,0:T(8,128)}, f32[256,256]{1,0:T(8,128)}), (f32[256,256]{1,0:T(8,128)}, f32[256,256]{1,0:T(8,128)})) %all-reduce.5.cloned.1.call-update) | async-done | bytes 524304 | tf_op jit(solution)/shard_map/psum | solution.py:104
  582.8 94.5 %all-reduce.7.cloned.1.call-done = (f32[64,256]{1,0:T(8,128)}, f32[64,256]{1,0:T(8,128)}) async-done(((f32[64,256]{1,0:T(8,128)}, f32[64,256]{1,0:T(8,128)}), (f32[64,256]{1,0:T(8,128)}, f32[64,256]{1,0:T(8,128)})) %all-reduce.7.cloned.1.call-update) | async-done | bytes 131088 | tf_op jit(solution)/shard_map/psum | solution.py:103
  677.3 1.5 copy.50
  678.7 1.5 copy.51
  680.2 1.7 copy.52
  681.9 1.7 copy.53
  (194 shorter events, 31.2 us)
Async XLA Ops:
  7.2 125.6 %copy-start = (bf16[1,1,256,256]{3,2,1,0:T(8,128)(2,1)S(1)}, bf16[1,1,256,256]{3,2,1,0:T(8,128)(2,1)}, u32[]{:S(2)}) copy-start(bf16[1,1,256,256]{3,2,1,0:T(8,128)(2,1)} %param.25) | copy-start | bytes 393220
  7.2 236.3 %reduce-scatter.2.cloned.1.call-start = ((), (), s32[]{:S(2)}) async-start(), calls=%async_computation.3 | async-start | bytes 5013504 | tf_op jit(solution)/shard_map/reduce_scatter | solution.py:49
  102.5 10.1 %copy-start.17 = (bf16[64,256]{1,0:T(8,128)(2,1)S(1)}, bf16[64,256]{1,0:T(8,128)(2,1)}, u32[]{:S(2)}) copy-start(bf16[64,256]{1,0:T(8,128)(2,1)} %param.16) | copy-start | bytes 98308
  112.7 1.3 copy-start.3
  112.7 1.6 copy-start.4
  112.7 2.0 copy-start.5
  112.7 2.3 copy-start.6
  112.7 2.7 copy-start.7
  112.7 3.0 copy-start.8
  112.7 3.3 copy-start.9
  112.7 3.7 copy-start.10
  112.8 4.0 copy-start.11
  116.7 11.3 %copy-start.18 = (bf16[64,256]{1,0:T(8,128)(2,1)S(1)}, bf16[64,256]{1,0:T(8,128)(2,1)}, u32[]{:S(2)}) copy-start(bf16[64,256]{1,0:T(8,128)(2,1)} %param.17) | copy-start | bytes 98308
  127.1 1.0 copy-start.1
  130.9 0.7 copy-start.50
  130.9 1.0 copy-start.16
  130.9 1.9 copy-start.14
  206.2 22.5 %all-to-all-start.1 = ((bf16[16,128,256]{2,1,0:T(8,128)(2,1)}), bf16[16,128,256]{2,1,0:T(8,128)(2,1)S(1)}, u32[]{:S(2)}, u32[]{:S(2)}) async-start(bf16[16,128,256]{2,1,0:T(8,128)(2,1)} %bitcast.53), calls=%async_computation.2 | async-start | bytes 2097152 | tf_op jit(solution)/shard_map/all_to_all | solution.py:90
  213.7 115.7 %all-gather.2.cloned.1.call-start = ((), (), s32[]{:S(2)}) async-start(), calls=%async_computation.4 | async-start | bytes 2506752 | tf_op jit(solution)/shard_map/all_gather | solution.py:98
  219.4 8.0 %copy-start.24 = (s32[256,1]{0,1:T(1,128)}, s32[256,1]{0,1:T(1,128)S(1)}, u32[]{:S(2)}) copy-start(s32[256,1]{0,1:T(1,128)S(1)} %get-tuple-element.51) | copy-start | bytes 3076
  219.4 8.0 %copy-start.26 = (s32[256,1]{0,1:T(1,128)}, s32[256,1]{0,1:T(1,128)S(1)}, u32[]{:S(2)}) copy-start(s32[256,1]{0,1:T(1,128)S(1)} %get-tuple-element.52) | copy-start | bytes 3076
  219.4 8.0 %copy-start.28 = (s32[256,1]{0,1:T(1,128)}, s32[256,1]{0,1:T(1,128)S(1)}, u32[]{:S(2)}) copy-start(s32[256,1]{0,1:T(1,128)S(1)} %get-tuple-element.49) | copy-start | bytes 3076
  219.4 8.0 %copy-start.30 = (s32[256,1]{0,1:T(1,128)}, s32[256,1]{0,1:T(1,128)S(1)}, u32[]{:S(2)}) copy-start(s32[256,1]{0,1:T(1,128)S(1)} %get-tuple-element.50) | copy-start | bytes 3076
  219.4 8.0 %copy-start.32 = (s32[256,1]{0,1:T(1,128)}, s32[256,1]{0,1:T(1,128)S(1)}, u32[]{:S(2)}) copy-start(s32[256,1]{0,1:T(1,128)S(1)} %get-tuple-element.47) | copy-start | bytes 3076
  219.4 8.0 %copy-start.34 = (s32[256,1]{0,1:T(1,128)}, s32[256,1]{0,1:T(1,128)S(1)}, u32[]{:S(2)}) copy-start(s32[256,1]{0,1:T(1,128)S(1)} %get-tuple-element.48) | copy-start | bytes 3076
  219.4 8.0 %copy-start.36 = (s32[256,1]{0,1:T(1,128)}, s32[256,1]{0,1:T(1,128)S(1)}, u32[]{:S(2)}) copy-start(s32[256,1]{0,1:T(1,128)S(1)} %get-tuple-element.45) | copy-start | bytes 3076
  219.4 8.0 %copy-start.38 = (s32[256,1]{0,1:T(1,128)}, s32[256,1]{0,1:T(1,128)S(1)}, u32[]{:S(2)}) copy-start(s32[256,1]{0,1:T(1,128)S(1)} %get-tuple-element.46) | copy-start | bytes 3076
  219.4 8.0 %copy-start.42 = (s32[256,1]{0,1:T(1,128)}, s32[256,1]{0,1:T(1,128)S(1)}, u32[]{:S(2)}) copy-start(s32[256,1]{0,1:T(1,128)S(1)} %get-tuple-element.42) | copy-start | bytes 3076
  228.7 1.0 copy-start.2
  240.8 4.5 copy-start.44
  240.8 5.1 copy-start.41
  240.8 5.7 copy-start.43
  240.8 6.3 copy-start.49
  240.8 6.3 copy-start.40
  240.8 6.3 copy-start.22
  240.8 6.3 copy-start.23
  240.8 6.8 copy-start.20
  240.8 6.8 copy-start.21
  240.8 7.9 %copy-start.37 = (s32[256,1]{0,1:T(1,128)S(1)}, s32[256,1]{0,1:T(1,128)}, u32[]{:S(2)}) copy-start(s32[256,1]{0,1:T(1,128)} %copy-done.36) | copy-start | bytes 3076
  240.9 7.9 %copy-start.39 = (s32[256,1]{0,1:T(1,128)S(1)}, s32[256,1]{0,1:T(1,128)}, u32[]{:S(2)}) copy-start(s32[256,1]{0,1:T(1,128)} %copy-done.38) | copy-start | bytes 3076
  240.9 8.5 %copy-start.33 = (s32[256,1]{0,1:T(1,128)S(1)}, s32[256,1]{0,1:T(1,128)}, u32[]{:S(2)}) copy-start(s32[256,1]{0,1:T(1,128)} %copy-done.32) | copy-start | bytes 3076
  240.9 8.5 %copy-start.35 = (s32[256,1]{0,1:T(1,128)S(1)}, s32[256,1]{0,1:T(1,128)}, u32[]{:S(2)}) copy-start(s32[256,1]{0,1:T(1,128)} %copy-done.34) | copy-start | bytes 3076
  240.9 9.0 %copy-start.19 = (s32[1,1,16,128]{3,2,1,0:T(8,128)S(1)}, s32[1,1,16,128]{3,2,1,0:T(8,128)}, u32[]{:S(2)}) copy-start(s32[1,1,16,128]{3,2,1,0:T(8,128)} %param.21) | copy-start | bytes 24580
  258.9 10.1 %copy-start.29 = (s32[256,1]{0,1:T(1,128)S(1)}, s32[256,1]{0,1:T(1,128)}, u32[]{:S(2)}) copy-start(s32[256,1]{0,1:T(1,128)} %copy-done.28) | copy-start | bytes 3076
  258.9 10.1 %copy-start.31 = (s32[256,1]{0,1:T(1,128)S(1)}, s32[256,1]{0,1:T(1,128)}, u32[]{:S(2)}) copy-start(s32[256,1]{0,1:T(1,128)} %copy-done.30) | copy-start | bytes 3076
  258.9 10.6 %copy-start.25 = (s32[256,1]{0,1:T(1,128)S(1)}, s32[256,1]{0,1:T(1,128)}, u32[]{:S(2)}) copy-start(s32[256,1]{0,1:T(1,128)} %copy-done.24) | copy-start | bytes 3076
  258.9 10.6 %copy-start.27 = (s32[256,1]{0,1:T(1,128)S(1)}, s32[256,1]{0,1:T(1,128)}, u32[]{:S(2)}) copy-start(s32[256,1]{0,1:T(1,128)} %copy-done.26) | copy-start | bytes 3076
  261.2 11.1 %copy-start.13 = (bf16[256,256]{1,0:T(8,128)(2,1)S(1)}, bf16[256,256]{1,0:T(8,128)(2,1)}, u32[]{:S(2)}) copy-start(bf16[256,256]{1,0:T(8,128)(2,1)} %param.18) | copy-start | bytes 393220
  261.2 21.7 %all-to-all-start = ((bf16[16,128,256]{2,1,0:T(8,128)(2,1)}), bf16[16,128,256]{2,1,0:T(8,128)(2,1)}, u32[]{:S(2)}, u32[]{:S(2)}) async-start(bf16[16,128,256]{2,1,0:T(8,128)(2,1)} %broadcast_select_fusion), calls=%async_computation.1 | async-start | bytes 2097152 | tf_op jit(solution)/shard_map/all_to_all | solution.py:60
  268.1 314.7 %all-reduce.5.cloned.1.call-start = ((), (), s32[]{:S(2)}) async-start(), calls=%async_computation.5 | async-start | bytes 1048576 | tf_op jit(solution)/shard_map/psum | solution.py:104
  313.9 12.5 %copy-start.45 = (pred[256]{0:T(512)(128)(4,1)S(1)}, pred[256]{0:T(512)(128)(4,1)}, u32[]{:S(2)}) copy-start(pred[256]{0:T(512)(128)(4,1)} %get-tuple-element.73) | copy-start | bytes 772
  313.9 12.5 %copy-start.46 = (pred[256]{0:T(512)(128)(4,1)S(1)}, pred[256]{0:T(512)(128)(4,1)}, u32[]{:S(2)}) copy-start(pred[256]{0:T(512)(128)(4,1)} %get-tuple-element.74) | copy-start | bytes 772
  313.9 12.5 %copy-start.47 = (pred[256]{0:T(512)(128)(4,1)S(1)}, pred[256]{0:T(512)(128)(4,1)}, u32[]{:S(2)}) copy-start(pred[256]{0:T(512)(128)(4,1)} %get-tuple-element.75) | copy-start | bytes 772
  313.9 12.5 %copy-start.48 = (pred[256]{0:T(512)(128)(4,1)S(1)}, pred[256]{0:T(512)(128)(4,1)}, u32[]{:S(2)}) copy-start(pred[256]{0:T(512)(128)(4,1)} %get-tuple-element.76) | copy-start | bytes 772
  329.3 347.9 %all-reduce.7.cloned.1.call-start = ((), (), s32[]{:S(2)}) async-start(), calls=%async_computation.6 | async-start | bytes 262144 | tf_op jit(solution)/shard_map/psum | solution.py:103
  329.4 3.3 copy-start.12
  332.7 1.3 copy-start.15
Sparse Core Ops, SparseCore 0:
  131.1 66.7 reduce-scatter.1
  245.4 42.2 all-gather.1
  329.5 253.2 all-reduce.4
  586.5 90.7 all-reduce.6
where the time goes:
time: 700 us; the launch traced here: 690 us
  waiting for transfers between devices  353 us (50%)
  local copies, waits for them, and re-layouts  172 us (25%)
  other arithmetic  122 us (17%)
  starting transfers between devices  14.8 us (2%)
  between operations  14.7 us (2%)
  matrix products  13.2 us (2%)
    psum x1, waiting for transfers between devices, per_device(): lax.psum((local_w2_self, local_w2_neigh), ('feat', 'dom'))  248 us
    gather x10, local copies, waits for them, and re-layouts, per_device(): jnp.take(feature_table, neigh_lists[column], axis=1).astype(jnp.float32)  101 us
    psum x1, waiting for transfers between devices, per_device(): first_self, first_mean = lax.psum((first_self, first_mean), 'dom')  94.5 us
    scatter-add x15, other arithmetic, per_device(): slot_sum = slot_sum.at[where_in[:, column]].add(d_mean)  70.3 us
    gather x17, local copies, waits for them, and re-layouts, rows_of(): return jnp.take(source_table, index_rows, axis=0)  53.6 us
    unnamed x108, local copies, waits for them, and re-layouts  15.1 us
  transfers between devices with their start and end apart: 6, of which 4 were waited for; matrix products, arithmetic and copies ran while one was open for 25% of the time, Pallas kernels for 0%

commit v1 on v0

--- a/solution.py
+++ b/solution.py
@@ -1,7 +1,17 @@
+import functools
 import jax
 import jax.numpy as jnp
 from jax import lax
 from jax.sharding import PartitionSpec as P
+
+
+def measure_the_pages(array_in, group_axis, device_axis):
+    for q in (group_axis, device_axis):
+        array_in = lax.psum(array_in, axis_name=q)
+    return array_in
+
+
+detail_steps_all = functools.partial(measure_the_pages, group_axis="feat", device_axis="dom")
 
 
 def rows_of(source_table, index_rows):
@@ -101,7 +111,7 @@
     first_self = jnp.dot(left_self, piece, preferred_element_type=jnp.float32)
     first_mean = jnp.dot(left_mean, piece, preferred_element_type=jnp.float32)
     first_self, first_mean = lax.psum((first_self, first_mean), "dom")
-    second_self, second_mean = lax.psum((local_w2_self, local_w2_neigh), ("feat", "dom"))
+    second_self, second_mean = detail_steps_all((local_w2_self, local_w2_neigh))
     return (layer_out[None, None], first_self, first_mean, second_self, second_mean)
 
 

time: 700 us -> 563 us (0.80)
  waiting for transfers between devices: 353 us -> 216 us
    psum x1, waiting for transfers between devices: 248 us -> 106 us  [measure_the_pages(): array_in = lax.psum(array_in, axis_name=q)]
    unnamed x108 -> x116, local copies, waits for them, and re-layouts: 15.1 us -> 15.1 us
  transfers between devices with their start and end apart: 6 -> 6, of which waited for: 4 -> 4; matrix products, arithmetic and copies ran while one was open for 25% -> 32% of each run, Pallas kernels for 0% -> 0%
where the time goes in v1:
time: 563 us; the launch traced here: 553 us
  waiting for transfers between devices  216 us (38%)
  local copies, waits for them, and re-layouts  171 us (30%)
  other arithmetic  124 us (22%)
  between operations  14.8 us (3%)
  starting transfers between devices  14.7 us (3%)
  matrix products  13.2 us (2%)
    psum x1, waiting for transfers between devices, measure_the_pages(): array_in = lax.psum(array_in, axis_name=q)  106 us
    gather x10, local copies, waits for them, and re-layouts, per_device(): jnp.take(feature_table, neigh_lists[column], axis=1).astype(jnp.float32)  101 us
    psum x1, waiting for transfers between devices, per_device(): first_self, first_mean = lax.psum((first_self, first_mean), 'dom')  99.1 us
    scatter-add x15, other arithmetic, per_device(): slot_sum = slot_sum.at[where_in[:, column]].add(d_mean)  70.3 us
    gather x17, local copies, waits for them, and re-layouts, rows_of(): return jnp.take(source_table, index_rows, axis=0)  52.9 us
    unnamed x116, local copies, waits for them, and re-layouts  15.1 us
  transfers between devices with their start and end apart: 6, of which 4 were waited for; matrix products, arithmetic and copies ran while one was open for 32% of the time, Pallas kernels for 0%

profile of v1, /device:TPU:2, one launch (start us, length us, event | category | flops | bytes accessed | tf_op | source)
XLA Modules:
  0.0 553.1 jit_solution(3701543779336192720)
XLA Ops:
  7.2 1.2 slice_reduce_fusion.9
  8.7 2.8 copy.24
  11.5 10.1 %gather_fusion.2 = bf16[4608,64]{1,0:T(8,128)(2,1)} fusion(bf16[64,9216]{0,1:T(8,128)(2,1)S(1)} %bitcast.99, s32[5120]{0:T(1024)S(1)} %pad_clamp_fusion.9), kind=kCustom, calls=%fused_computation.clone | custom fusion | bytes 1198080 | tf_op jit(solution)/shard_map/jit(_take)/gather | solution.py:52
  21.6 10.1 %gather_fusion.3 = bf16[4608,64]{1,0:T(8,128)(2,1)} fusion(bf16[64,9216]{0,1:T(8,128)(2,1)S(1)} %bitcast.100, s32[5120]{0:T(1024)S(1)} %pad_clamp_fusion.8), kind=kCustom, calls=%fused_computation.2.clone | custom fusion | bytes 1198080 | tf_op jit(solution)/shard_map/jit(_take)/gather | solution.py:52
  31.7 10.1 %gather_fusion.4 = bf16[4608,64]{1,0:T(8,128)(2,1)} fusion(bf16[64,9216]{0,1:T(8,128)(2,1)S(1)} %bitcast.101, s32[5120]{0:T(1024)S(1)} %pad_clamp_fusion.7), kind=kCustom, calls=%fused_computation.3.clone | custom fusion | bytes 1198080 | tf_op jit(solution)/shard_map/jit(_take)/gather | solution.py:52
  41.8 10.1 %gather_fusion.5 = bf16[4608,64]{1,0:T(8,128)(2,1)} fusion(bf16[64,9216]{0,1:T(8,128)(2,1)S(1)} %bitcast.102, s32[5120]{0:T(1024)S(1)} %pad_clamp_fusion.6), kind=kCustom, calls=%fused_computation.4.clone | custom fusion | bytes 1198080 | tf_op jit(solution)/shard_map/jit(_take)/gather | solution.py:52
  51.9 10.1 %gather_fusion.6 = bf16[4608,64]{1,0:T(8,128)(2,1)} fusion(bf16[64,9216]{0,1:T(8,128)(2,1)S(1)} %bitcast.103, s32[5120]{0:T(1024)S(1)} %pad_clamp_fusion.5), kind=kCustom, calls=%fused_computation.5.clone | custom fusion | bytes 1198080 | tf_op jit(solution)/shard_map/jit(_take)/gather | solution.py:52
  62.1 10.1 %gather_fusion.7 = bf16[4608,64]{1,0:T(8,128)(2,1)} fusion(bf16[64,9216]{0,1:T(8,128)(2,1)S(1)} %bitcast.104, s32[5120]{0:T(1024)S(1)} %pad_clamp_fusion.4), kind=kCustom, calls=%fused_computation.6.clone | custom fusion | bytes 1198080 | tf_op jit(solution)/shard_map/jit(_take)/gather | solution.py:52
  72.2 10.1 %gather_fusion.8 = bf16[4608,64]{1,0:T(8,128)(2,1)} fusion(bf16[64,9216]{0,1:T(8,128)(2,1)S(1)} %bitcast.105, s32[5120]{0:T(1024)S(1)} %pad_clamp_fusion.3), kind=kCustom, calls=%fused_computation.7.clone | custom fusion | bytes 1198080 | tf_op jit(solution)/shard_map/jit(_take)/gather | solution.py:52
  82.3 10.1 %gather_fusion.9 = bf16[4608,64]{1,0:T(8,128)(2,1)} fusion(bf16[64,9216]{0,1:T(8,128)(2,1)S(1)} %bitcast.106, s32[5120]{0:T(1024)S(1)} %pad_clamp_fusion.2), kind=kCustom, calls=%fused_computation.8.clone | custom fusion | bytes 1198080 | tf_op jit(solution)/shard_map/jit(_take)/gather | solution.py:52
  92.4 10.1 %gather_fusion.10 = bf16[4608,64]{1,0:T(8,128)(2,1)} fusion(bf16[64,9216]{0,1:T(8,128)(2,1)S(1)} %bitcast.107, s32[5120]{0:T(1024)S(1)} %pad_clamp_fusion.1), kind=kCustom, calls=%fused_computation.9.clone | custom fusion | bytes 1198080 | tf_op jit(solution)/shard_map/jit(_take)/gather | solution.py:52
  102.6 10.1 %gather_fusion.11 = bf16[4608,64]{1,0:T(8,128)(2,1)} fusion(bf16[64,9216]{0,1:T(8,128)(2,1)S(1)} %bitcast.108, s32[5120]{0:T(1024)S(1)} %pad_clamp_fusion), kind=kCustom, calls=%fused_computation.10.clone | custom fusion | bytes 1198080 | tf_op jit(solution)/shard_map/jit(_take)/gather | solution.py:52
  116.8 10.3 %multiply_convert_fusion = bf16[64,4608]{0,1:T(8,128)(2,1)S(1)} fusion(bf16[4608,64]{1,0:T(8,128)(2,1)} %gather_fusion.11, bf16[4608,64]{1,0:T(8,128)(2,1)S(1)} %copy-done.11, bf16[4608,64]{1,0:T(8,128)(2,1)S(1)} %copy-done.10, bf16[4608,64]{1,0:T(8,128)(2,1)S(1)} %copy-done.9, bf16[4608,64]{1,0:T(8,128)(2,1)S(1)} %copy-done.8, ...), kind=kLoop, calls=%fused_computation.45 | loop fusion | flops 9142272 | bytes 6534144 | tf_op jit(solution)/shard_map/convert_element_type | solution.py:53
  128.1 2.9 convolution_add_fusion
  133.0 3.4 scatter_custom_fusion
  136.4 4.7 scatter_fusion
  141.2 5.2 scatter_fusion.1
  146.3 4.7 scatter_fusion.2
  151.1 4.8 scatter_fusion.3
  155.8 4.7 scatter_fusion.4
  160.6 4.7 scatter_fusion.5
  165.3 4.8 scatter_fusion.6
  170.1 4.8 scatter_fusion.7
  174.8 4.7 scatter_fusion.8
  179.5 4.8 scatter_fusion.9
  184.3 4.8 scatter_fusion.10
  189.1 4.9 scatter_fusion.11
  194.0 4.7 scatter_fusion.12
  198.7 4.7 scatter_fusion.13
  203.4 2.8 convert_element_type.133
  206.2 7.5 %all-to-all-start.1 = ((bf16[16,128,256]{2,1,0:T(8,128)(2,1)}), bf16[16,128,256]{2,1,0:T(8,128)(2,1)S(1)}, u32[]{:S(2)}, u32[]{:S(2)}) async-start(bf16[16,128,256]{2,1,0:T(8,128)(2,1)} %bitcast.53), calls=%async_computation.2 | async-start | bytes 2097152 | tf_op jit(solution)/shard_map/all_to_all | solution.py:100
  225.5 1.8 fusion.18
  229.7 11.0 %scatter_custom_fusion.15 = f32[288,256]{1,0:T(8,128)S(1)} fusion(s32[2048]{0:T(1024)S(1)} %bitcast.115, bf16[2048,256]{1,0:T(8,128)(2,1)} %bitcast.111, f32[]{:T(128)} %constant.47.clone.1), kind=kCustom, calls=%fused_computation.46 | custom fusion | flops 1048576 | bytes 1343492 | tf_op jit(solution)/shard_map/scatter-add | solution.py:102
  240.9 2.5 scatter_fusion.14
  243.4 1.8 fusion.12
  250.5 9.0 %gather_fusion.1 = bf16[2048,256]{1,0:T(8,128)(2,1)} fusion(bf16[288,256]{1,0:T(8,128)(2,1)S(1)} %get-tuple-element.24, s32[2048]{0:T(1024)S(1)} %broadcast_clamp_fusion), kind=kCustom, calls=%fused_computation.26 | custom fusion | bytes 2105344 | tf_op jit(solution)/shard_map/jit(_take)/gather | solution.py:18
  259.5 2.3 broadcast_select_fusion
  261.8 6.8 %all-to-all-start = ((bf16[16,128,256]{2,1,0:T(8,128)(2,1)}), bf16[16,128,256]{2,1,0:T(8,128)(2,1)}, u32[]{:S(2)}, u32[]{:S(2)}) async-start(bf16[16,128,256]{2,1,0:T(8,128)(2,1)} %broadcast_select_fusion), calls=%async_computation.1 | async-start | bytes 2097152 | tf_op jit(solution)/shard_map/all_to_all | solution.py:70
  271.2 1.3 gather_fusion
  273.5 9.9 %all-to-all-done = bf16[16,128,256]{2,1,0:T(8,128)(2,1)} async-done(((bf16[16,128,256]{2,1,0:T(8,128)(2,1)}), bf16[16,128,256]{2,1,0:T(8,128)(2,1)}, u32[]{:S(2)}, u32[]{:S(2)}) %all-to-all-start) | async-done | bytes 1048608 | tf_op jit(solution)/shard_map/all_to_all | solution.py:70
  283.4 2.5 gather_fusion.23
  285.9 2.5 gather_fusion.24
  288.4 2.5 gather_fusion.25
  290.8 2.5 gather_fusion.26
  293.3 2.3 gather_fusion.12
  295.6 2.5 gather_fusion.13
  298.1 3.1 gather_fusion.14
  301.2 3.1 gather_fusion.15
  304.3 3.1 gather_fusion.16
  307.4 3.1 gather_fusion.17
  310.5 3.1 gather_fusion.18
  313.7 3.1 gather_fusion.19
  316.8 3.1 gather_fusion.20
  319.9 3.1 gather_fusion.21
  323.0 3.1 gather_fusion.22
  326.1 2.0 multiply_convert_fusion.1
  329.2 3.3 fusion.25
  332.5 1.3 convolution_bitcast_fusion
  333.8 106.0 %all-reduce.7.cloned.1.call-done = (f32[256,256]{1,0:T(8,128)}, f32[256,256]{1,0:T(8,128)}) async-done(((f32[256,256]{1,0:T(8,128)}, f32[256,256]{1,0:T(8,128)}), (f32[256,256]{1,0:T(8,128)}, f32[256,256]{1,0:T(8,128)})) %all-reduce.7.cloned.1.call-update) | async-done | bytes 524304 | tf_op jit(solution)/shard_map/psum | solution.py:10
  440.9 99.1 %all-reduce.5.cloned.1.call-done = (f32[64,256]{1,0:T(8,128)}, f32[64,256]{1,0:T(8,128)}, f32[256,256]{1,0:T(8,128)}, f32[256,256]{1,0:T(8,128)}) async-done(((f32[64,256]{1,0:T(8,128)}, f32[64,256]{1,0:T(8,128)}, f32[256,256]{1,0:T(8,128)}, f32[256,256]{1,0:T(8,128)}), (f32[64,256]{1,0:T(8,128)}, f32[64,256]{1,0:T(8,128)}, f32[256,256]{1,0:T(8,128)}, f32[256,256]{1,0:T(8,128)})) %all-reduce.5.cloned.1.call-update) | async-done | bytes 655376 | tf_op jit(solution)/shard_map/psum | solution.py:113
  540.0 1.5 copy.52
  541.5 1.5 copy.53
  543.0 1.7 copy.54
  544.6 1.7 copy.55
  (202 shorter events, 32.4 us)
Async XLA Ops:
  7.2 125.6 %copy-start = (bf16[1,1,256,256]{3,2,1,0:T(8,128)(2,1)S(1)}, bf16[1,1,256,256]{3,2,1,0:T(8,128)(2,1)}, u32[]{:S(2)}) copy-start(bf16[1,1,256,256]{3,2,1,0:T(8,128)(2,1)} %param.25) | copy-start | bytes 393220
  7.2 236.3 %reduce-scatter.2.cloned.1.call-start = ((), (), s32[]{:S(2)}) async-start(), calls=%async_computation.3 | async-start | bytes 5013504 | tf_op jit(solution)/shard_map/reduce_scatter | solution.py:59
  102.5 10.1 %copy-start.17 = (bf16[64,256]{1,0:T(8,128)(2,1)S(1)}, bf16[64,256]{1,0:T(8,128)(2,1)}, u32[]{:S(2)}) copy-start(bf16[64,256]{1,0:T(8,128)(2,1)} %param.16) | copy-start | bytes 98308
  112.7 1.3 copy-start.3
  112.7 1.6 copy-start.4
  112.7 2.0 copy-start.5
  112.7 2.3 copy-start.6
  112.7 2.7 copy-start.7
  112.7 3.0 copy-start.8
  112.7 3.3 copy-start.9
  112.7 3.7 copy-start.10
  112.8 4.0 copy-start.11
  116.7 11.3 %copy-start.18 = (bf16[64,256]{1,0:T(8,128)(2,1)S(1)}, bf16[64,256]{1,0:T(8,128)(2,1)}, u32[]{:S(2)}) copy-start(bf16[64,256]{1,0:T(8,128)(2,1)} %param.17) | copy-start | bytes 98308
  127.1 1.0 copy-start.1
  130.9 0.7 copy-start.54
  130.9 1.0 copy-start.16
  130.9 1.9 copy-start.14
  206.2 22.5 %all-to-all-start.1 = ((bf16[16,128,256]{2,1,0:T(8,128)(2,1)}), bf16[16,128,256]{2,1,0:T(8,128)(2,1)S(1)}, u32[]{:S(2)}, u32[]{:S(2)}) async-start(bf16[16,128,256]{2,1,0:T(8,128)(2,1)} %bitcast.53), calls=%async_computation.2 | async-start | bytes 2097152 | tf_op jit(solution)/shard_map/all_to_all | solution.py:100
  213.7 115.5 %all-gather.2.cloned.1.call-start = ((), (), s32[]{:S(2)}) async-start(), calls=%async_computation.4 | async-start | bytes 2506752 | tf_op jit(solution)/shard_map/all_gather | solution.py:108
  219.4 8.0 %copy-start.24 = (s32[256,1]{0,1:T(1,128)}, s32[256,1]{0,1:T(1,128)S(1)}, u32[]{:S(2)}) copy-start(s32[256,1]{0,1:T(1,128)S(1)} %get-tuple-element.53) | copy-start | bytes 3076
  219.4 8.0 %copy-start.26 = (s32[256,1]{0,1:T(1,128)}, s32[256,1]{0,1:T(1,128)S(1)}, u32[]{:S(2)}) copy-start(s32[256,1]{0,1:T(1,128)S(1)} %get-tuple-element.54) | copy-start | bytes 3076
  219.4 8.0 %copy-start.28 = (s32[256,1]{0,1:T(1,128)}, s32[256,1]{0,1:T(1,128)S(1)}, u32[]{:S(2)}) copy-start(s32[256,1]{0,1:T(1,128)S(1)} %get-tuple-element.51) | copy-start | bytes 3076
  219.4 8.0 %copy-start.30 = (s32[256,1]{0,1:T(1,128)}, s32[256,1]{0,1:T(1,128)S(1)}, u32[]{:S(2)}) copy-start(s32[256,1]{0,1:T(1,128)S(1)} %get-tuple-element.52) | copy-start | bytes 3076
  219.4 8.0 %copy-start.32 = (s32[256,1]{0,1:T(1,128)}, s32[256,1]{0,1:T(1,128)S(1)}, u32[]{:S(2)}) copy-start(s32[256,1]{0,1:T(1,128)S(1)} %get-tuple-element.49) | copy-start | bytes 3076
  219.4 8.0 %copy-start.34 = (s32[256,1]{0,1:T(1,128)}, s32[256,1]{0,1:T(1,128)S(1)}, u32[]{:S(2)}) copy-start(s32[256,1]{0,1:T(1,128)S(1)} %get-tuple-element.50) | copy-start | bytes 3076
  219.4 8.0 %copy-start.36 = (s32[256,1]{0,1:T(1,128)}, s32[256,1]{0,1:T(1,128)S(1)}, u32[]{:S(2)}) copy-start(s32[256,1]{0,1:T(1,128)S(1)} %get-tuple-element.47) | copy-start | bytes 3076
  219.4 8.0 %copy-start.38 = (s32[256,1]{0,1:T(1,128)}, s32[256,1]{0,1:T(1,128)S(1)}, u32[]{:S(2)}) copy-start(s32[256,1]{0,1:T(1,128)S(1)} %get-tuple-element.48) | copy-start | bytes 3076
  219.4 8.0 %copy-start.42 = (s32[256,1]{0,1:T(1,128)}, s32[256,1]{0,1:T(1,128)S(1)}, u32[]{:S(2)}) copy-start(s32[256,1]{0,1:T(1,128)S(1)} %get-tuple-element.44) | copy-start | bytes 3076
  228.7 1.0 copy-start.2
  240.8 4.5 copy-start.46
  240.8 5.1 copy-start.44
  240.8 5.7 %copy-start.45 = (s32[256]{0:T(256)S(1)}, s32[256]{0:T(256)}, u32[]{:S(2)}) copy-start(s32[256]{0:T(256)} %compare_select_fusion.37) | copy-start | bytes 3076
  240.8 6.3 %copy-start.41 = (s32[256,1]{0,1:T(1,128)S(1)}, s32[256,1]{0,1:T(1,128)}, u32[]{:S(2)}) copy-start(s32[256,1]{0,1:T(1,128)} %get-tuple-element.46) | copy-start | bytes 3076
  240.8 6.9 %copy-start.43 = (s32[256,1]{0,1:T(1,128)S(1)}, s32[256,1]{0,1:T(1,128)}, u32[]{:S(2)}) copy-start(s32[256,1]{0,1:T(1,128)} %copy-done.42) | copy-start | bytes 3076
  240.8 7.4 %copy-start.53 = (s32[1,1,256]{2,1,0:T(1,128)S(1)}, s32[1,1,256]{2,1,0:T(1,128)}, u32[]{:S(2)}) copy-start(s32[1,1,256]{2,1,0:T(1,128)} %param.24) | copy-start | bytes 3076
  240.8 7.4 %copy-start.40 = (s32[256,1]{0,1:T(1,128)S(1)}, s32[256,1]{0,1:T(1,128)}, u32[]{:S(2)}) copy-start(s32[256,1]{0,1:T(1,128)} %get-tuple-element.45) | copy-start | bytes 3076
  240.8 7.4 %copy-start.22 = (s32[256,1]{0,1:T(1,128)S(1)}, s32[256,1]{0,1:T(1,128)}, u32[]{:S(2)}) copy-start(s32[256,1]{0,1:T(1,128)} %get-tuple-element.40) | copy-start | bytes 3076
  240.8 7.4 %copy-start.23 = (s32[256,1]{0,1:T(1,128)S(1)}, s32[256,1]{0,1:T(1,128)}, u32[]{:S(2)}) copy-start(s32[256,1]{0,1:T(1,128)} %get-tuple-element.41) | copy-start | bytes 3076
  240.8 8.0 %copy-start.20 = (s32[256,1]{0,1:T(1,128)S(1)}, s32[256,1]{0,1:T(1,128)}, u32[]{:S(2)}) copy-start(s32[256,1]{0,1:T(1,128)} %get-tuple-element.42) | copy-start | bytes 3076
  240.9 8.0 %copy-start.21 = (s32[256,1]{0,1:T(1,128)S(1)}, s32[256,1]{0,1:T(1,128)}, u32[]{:S(2)}) copy-start(s32[256,1]{0,1:T(1,128)} %get-tuple-element.43) | copy-start | bytes 3076
  240.9 9.1 %copy-start.37 = (s32[256,1]{0,1:T(1,128)S(1)}, s32[256,1]{0,1:T(1,128)}, u32[]{:S(2)}) copy-start(s32[256,1]{0,1:T(1,128)} %copy-done.36) | copy-start | bytes 3076
  240.9 9.1 %copy-start.39 = (s32[256,1]{0,1:T(1,128)S(1)}, s32[256,1]{0,1:T(1,128)}, u32[]{:S(2)}) copy-start(s32[256,1]{0,1:T(1,128)} %copy-done.38) | copy-start | bytes 3076
  240.9 9.6 %copy-start.19 = (s32[1,1,16,128]{3,2,1,0:T(8,128)S(1)}, s32[1,1,16,128]{3,2,1,0:T(8,128)}, u32[]{:S(2)}) copy-start(s32[1,1,16,128]{3,2,1,0:T(8,128)} %param.21) | copy-start | bytes 24580
  248.2 24.3 %copy-start.47 = (pred[256]{0:T(512)(128)(4,1)}, pred[256]{0:T(512)(128)(4,1)S(1)}, u32[]{:S(2)}) copy-start(pred[256]{0:T(512)(128)(4,1)S(1)} %compare_and_fusion.26) | copy-start | bytes 772
  259.5 10.0 %copy-start.33 = (s32[256,1]{0,1:T(1,128)S(1)}, s32[256,1]{0,1:T(1,128)}, u32[]{:S(2)}) copy-start(s32[256,1]{0,1:T(1,128)} %copy-done.32) | copy-start | bytes 3076
  259.5 10.0 %copy-start.35 = (s32[256,1]{0,1:T(1,128)S(1)}, s32[256,1]{0,1:T(1,128)}, u32[]{:S(2)}) copy-start(s32[256,1]{0,1:T(1,128)} %copy-done.34) | copy-start | bytes 3076
  259.5 10.5 %copy-start.29 = (s32[256,1]{0,1:T(1,128)S(1)}, s32[256,1]{0,1:T(1,128)}, u32[]{:S(2)}) copy-start(s32[256,1]{0,1:T(1,128)} %copy-done.28) | copy-start | bytes 3076
  259.5 10.5 %copy-start.31 = (s32[256,1]{0,1:T(1,128)S(1)}, s32[256,1]{0,1:T(1,128)}, u32[]{:S(2)}) copy-start(s32[256,1]{0,1:T(1,128)} %copy-done.30) | copy-start | bytes 3076
  259.5 11.1 %copy-start.25 = (s32[256,1]{0,1:T(1,128)S(1)}, s32[256,1]{0,1:T(1,128)}, u32[]{:S(2)}) copy-start(s32[256,1]{0,1:T(1,128)} %copy-done.24) | copy-start | bytes 3076
  259.5 11.1 %copy-start.27 = (s32[256,1]{0,1:T(1,128)S(1)}, s32[256,1]{0,1:T(1,128)}, u32[]{:S(2)}) copy-start(s32[256,1]{0,1:T(1,128)} %copy-done.26) | copy-start | bytes 3076
  261.8 21.6 %all-to-all-start = ((bf16[16,128,256]{2,1,0:T(8,128)(2,1)}), bf16[16,128,256]{2,1,0:T(8,128)(2,1)}, u32[]{:S(2)}, u32[]{:S(2)}) async-start(bf16[16,128,256]{2,1,0:T(8,128)(2,1)} %broadcast_select_fusion), calls=%async_computation.1 | async-start | bytes 2097152 | tf_op jit(solution)/shard_map/all_to_all | solution.py:70
  268.6 171.2 %all-reduce.7.cloned.1.call-start = ((), (), s32[]{:S(2)}) async-start(), calls=%async_computation.6 | async-start | bytes 1048576 | tf_op jit(solution)/shard_map/psum | solution.py:10
  313.6 12.5 %copy-start.49 = (pred[256]{0:T(512)(128)(4,1)S(1)}, pred[256]{0:T(512)(128)(4,1)}, u32[]{:S(2)}) copy-start(pred[256]{0:T(512)(128)(4,1)} %get-tuple-element.75) | copy-start | bytes 772
  313.6 12.5 %copy-start.50 = (pred[256]{0:T(512)(128)(4,1)S(1)}, pred[256]{0:T(512)(128)(4,1)}, u32[]{:S(2)}) copy-start(pred[256]{0:T(512)(128)(4,1)} %get-tuple-element.76) | copy-start | bytes 772
  313.6 12.5 %copy-start.51 = (pred[256]{0:T(512)(128)(4,1)S(1)}, pred[256]{0:T(512)(128)(4,1)}, u32[]{:S(2)}) copy-start(pred[256]{0:T(512)(128)(4,1)} %get-tuple-element.77) | copy-start | bytes 772
  313.7 12.5 %copy-start.52 = (pred[256]{0:T(512)(128)(4,1)S(1)}, pred[256]{0:T(512)(128)(4,1)}, u32[]{:S(2)}) copy-start(pred[256]{0:T(512)(128)(4,1)} %get-tuple-element.78) | copy-start | bytes 772
  329.1 210.9 %all-reduce.5.cloned.1.call-start = ((), (), s32[]{:S(2)}) async-start(), calls=%async_computation.5 | async-start | bytes 1310720 | tf_op jit(solution)/shard_map/psum | solution.py:113
  329.2 3.3 copy-start.12
  332.5 107.3 %copy-start.13 = (bf16[256,256]{1,0:T(8,128)(2,1)S(1)}, bf16[256,256]{1,0:T(8,128)(2,1)}, u32[]{:S(2)}) copy-start(bf16[256,256]{1,0:T(8,128)(2,1)} %param.18) | copy-start | bytes 393220
  332.5 107.3 %copy-start.48 = (pred[256]{0:T(512)(128)(4,1)S(1)}, pred[256]{0:T(512)(128)(4,1)}, u32[]{:S(2)}) copy-start(pred[256]{0:T(512)(128)(4,1)} %copy-done.47) | copy-start | bytes 772
  332.5 107.6 %copy-start.15 = (bf16[256,256]{1,0:T(8,128)(2,1)S(1)}, bf16[256,256]{1,0:T(8,128)(2,1)}, u32[]{:S(2)}) copy-start(bf16[256,256]{1,0:T(8,128)(2,1)} %param.19) | copy-start | bytes 393220
Sparse Core Ops, SparseCore 0:
  131.1 66.7 reduce-scatter.1
  245.4 42.1 all-gather.1
  329.2 110.5 all-reduce.6
  444.3 95.7 all-reduce.4
